TPU v7x, 32 devices: a whole 2x2x4 slice. The times are simulated.
32 devices in a mesh: groups: 2 (over y), vocab: 4 (over z), edit: 2 (over x), tok: 2 (over core).
Axes of the slice: x: 2, y: 2, z: 4, core: 2. Of those that a mesh axis runs over, the one named last changes fastest.
Arguments:
- token_ids: int32 [256], P(('groups', 'tok')), parts along dimension 0, may hold values from 0 to 4095
- valid_mask: int32 [256], P(('groups', 'tok')), parts along dimension 0, may hold values 0 or 1
- key_index: int32 [4], P('groups'), parts along dimension 0, may hold values from 0 to 3
- hidden_act: bfloat16 [256, 14336], P(('groups', 'tok'), 'vocab'), parts along dimension 0, may hold values from -6 to 6
- key_table: bfloat16 [4, 14336], P(None, 'vocab'), may hold values from -0.046875 to 0.046875
- base_out: bfloat16 [256, 4096], P(('groups', 'tok'), 'vocab'), parts along dimension 0, may hold values from -50 to 50
- value_vecs: bfloat16 [4, 4096], P(('groups', 'edit'), 'vocab'), parts along dimension 0, may hold values from -6 to 6
- norm_gain: float32 [4096], replicated, may hold values from 0.5 to 1.5
- head: bfloat16 [4096, 4096], P(('vocab', 'edit')), may hold values from -46 to 46
Outputs:
- grad_value: float32 [4, 4096], P(('groups', 'edit'), 'vocab'), parts along dimension 0
- token_kl: float32 [4, 128], P(('groups', 'edit'), 'tok'), parts along dimension 0
- target_logprob: float32 [4, 128], P(('groups', 'edit'), 'tok'), parts along dimension 0
There are 2 independent parts, one for each index of `groups`. A program takes and returns all parts, laid end to end along the dimension named above; an argument that names none is the same for every part. Nothing has to cross between parts.
All inputs are finite; a program needn't handle non-finite values. No bound on the sum of `valid_mask` on one device may be relied on, other than what follows from the above.
Results may differ from a plain program's by a relative error of at most 0.0061.
Values may be sent and summed in bfloat16 or wider, within the bound.
A program may use at most 64 MiB of HBM per device.

v0:
```python
import jax
import jax.numpy as jnp
from jax import lax
from jax.sharding import PartitionSpec as P

NORM_EPS = 1e-05


def rms_scale(hidden_rows):
    return lax.rsqrt(jnp.mean(hidden_rows * hidden_rows, axis=-1, keepdims=True) + NORM_EPS)


def per_device(
    token_ids, valid_mask, key_index, hidden_act, key_table, base_out, value_vecs, norm_gain, head
):
    vocab_rows = head.shape[0]
    edit_rows = value_vecs.shape[0]
    piece_width = value_vecs.shape[1]
    key_slots = jnp.arange(key_table.shape[0], dtype=jnp.int32)
    select = (key_index[:, None] == key_slots[None, :]).astype(jnp.bfloat16)
    edit_keys = jnp.dot(select, key_table, preferred_element_type=jnp.float32).astype(jnp.bfloat16)
    coeff_part = lax.dot_general(
        edit_keys, hidden_act, (((1,), (1,)), ((), ())), preferred_element_type=jnp.float32
    )
    coeff = lax.psum(coeff_part, "vocab")
    base_rows, local_values = (
        lax.all_gather(base_out, "vocab", axis=1, tiled=True),
        lax.all_gather(value_vecs, "vocab", axis=1, tiled=True),
    )
    values = lax.all_gather(local_values, "edit", axis=0, tiled=True)
    base32 = base_rows.astype(jnp.float32)
    base_norm = (norm_gain * base32 * rms_scale(base32)).astype(jnp.bfloat16)
    base_logits = lax.dot_general(
        base_norm, head, (((1,), (1,)), ((), ())), preferred_element_type=jnp.float32
    )
    edited = base32[None, :, :] + coeff[:, :, None] * values.astype(jnp.float32)[:, None, :]
    row_scale = rms_scale(edited)
    normed = (norm_gain * edited * row_scale).astype(jnp.bfloat16)
    logits = jnp.einsum("etd,vd->etv", normed, head, preferred_element_type=jnp.float32)
    vocab_start = lax.axis_index(("vocab", "edit")) * vocab_rows
    vocab_ids = vocab_start + jnp.arange(vocab_rows, dtype=jnp.int32)
    onehot = (token_ids[:, None] == vocab_ids[None, :]).astype(jnp.float32)
    peak_base = jnp.max(base_logits, axis=-1)
    peak_edit = jnp.max(logits, axis=-1)
    peak_base, peak_edit = lax.pmax((peak_base, peak_edit), ("vocab", "edit"))
    base_exp = jnp.exp(base_logits - peak_base[:, None])
    base_total = jnp.sum(base_exp, axis=-1)
    edit_total = jnp.sum(jnp.exp(logits - peak_edit[:, :, None]), axis=-1)
    cross_sum = jnp.sum(base_exp[None, :, :] * (base_logits[None, :, :] - logits), axis=-1)
    target = jnp.sum(onehot[None, :, :] * logits, axis=-1)
    base_total, edit_total, cross_sum, target = lax.psum(
        (base_total, edit_total, cross_sum, target), ("vocab", "edit")
    )
    base_lse = peak_base + jnp.log(base_total)
    edit_lse = peak_edit + jnp.log(edit_total)
    valid = valid_mask.astype(jnp.float32)
    token_kl = valid[None, :] * (cross_sum / base_total[None, :] - base_lse[None, :] + edit_lse)
    target_logprob = target - edit_lse
    base_prob = jnp.exp(base_logits - base_lse[:, None])
    edit_prob = jnp.exp(logits - edit_lse[:, :, None])
    logit_grad = (valid[None, :, None] * (edit_prob - base_prob[None, :, :])).astype(jnp.bfloat16)
    back_rows = jnp.einsum("etv,vd->etd", logit_grad, head, preferred_element_type=jnp.float32)
    grad_y = norm_gain * back_rows
    grad_o = row_scale * grad_y - edited * row_scale**3 * jnp.mean(
        grad_y * edited, axis=-1, keepdims=True
    )
    grad_part = jnp.sum(coeff[:, :, None] * grad_o, axis=1)
    edit_start = lax.axis_index("edit") * edit_rows
    grad_total = lax.psum(grad_part, ("vocab", "edit", "tok"))
    grad_mine = lax.dynamic_slice_in_dim(grad_total, edit_start, edit_rows, 0)
    grad_piece = lax.dynamic_slice_in_dim(
        grad_mine, lax.axis_index("vocab") * piece_width, piece_width, 1
    )
    kl_mine = lax.dynamic_slice_in_dim(token_kl, edit_start, edit_rows, 0)
    target_mine = lax.dynamic_slice_in_dim(target_logprob, edit_start, edit_rows, 0)
    return (grad_piece, kl_mine, target_mine)


def solution(mesh):
    placed = (
        P(("groups", "tok")),
        P(("groups", "tok")),
        P("groups"),
        P(("groups", "tok"), "vocab"),
        P(None, "vocab"),
        P(("groups", "tok"), "vocab"),
        P(("groups", "edit"), "vocab"),
        P(),
        P(("vocab", "edit"), None),
    )
    return jax.shard_map(
        per_device,
        mesh=mesh,
        in_specs=placed,
        out_specs=(
            P(("groups", "edit"), "vocab"),
            P(("groups", "edit"), "tok"),
            P(("groups", "edit"), "tok"),
        ),
        check_vma=False,
    )
```

profile of v0, /device:TPU:0, one launch (start us, length us, event | category | flops | bytes accessed | tf_op | source)
XLA Modules:
  0.0 156.0 jit_solution(18408327459742363050)
XLA Ops:
  0.6 0.0 copy-start
  0.7 0.7 convert_element_type.32
  1.4 0.3 copy-done
  1.7 1.1 fusion.3
  2.8 13.4 %psum.42 = f32[2,64]{1,0:T(2,128)S(1)} all-reduce(f32[2,64]{1,0:T(2,128)S(1)} %fusion.3), channel_id=1, replica_groups=mesh['groups'=2,'vocab'=4,'edit'=2,'tok'=2] {'vocab'}, use_global_device_ids=true, to_apply=%region_0.0 | all-reduce | flops 128 | bytes 1024 | tf_op jit(solution)/shard_map/psum | solution.py:25
  16.3 13.3 %all_gather.10 = bf16[1,4096]{1,0:T(2,128)(2,1)S(1)} all-gather(bf16[1,1024]{1,0:T(2,128)(2,1)} %param.15), channel_id=1, replica_groups=mesh['groups'=2,'vocab'=4,'edit'=2,'tok'=2] {'vocab'}, dimensions={1}, use_global_device_ids=true | all-gather | bytes 10240 | tf_op jit(solution)/shard_map/all_gather | solution.py:28
  29.5 4.4 %all-gather = bf16[2,1,4096]{2,1,0:T(2,128)(2,1)S(1)} all-gather(bf16[1,1,4096]{2,1,0:T(2,128)(2,1)S(1)} %bitcast.20), channel_id=1, replica_groups=mesh['groups'=2,'vocab'=4,'edit'=2,'tok'=2] {'edit'}, dimensions={0}, use_global_device_ids=true | all-gather | bytes 24576 | tf_op jit(solution)/shard_map/all_gather | solution.py:30
  34.0 0.7 compare_convert_fusion
  34.7 15.0 %all_gather.9 = bf16[64,4096]{1,0:T(8,128)(2,1)S(1)} all-gather(bf16[64,1024]{1,0:T(8,128)(2,1)} %param.14), channel_id=1, replica_groups=mesh['groups'=2,'vocab'=4,'edit'=2,'tok'=2] {'vocab'}, dimensions={1}, use_global_device_ids=true | all-gather | bytes 655360 | tf_op jit(solution)/shard_map/all_gather | solution.py:27
  49.7 0.2 multiply_reduce_fusion.3
  49.9 0.0 copy-start.1
  49.9 3.9 %fusion.24 = (f32[64]{0:T(128)S(1)}, f32[64,512]{1,0:T(8,128)S(1)}) fusion(bf16[512,4096]{1,0:T(8,128)(2,1)} %param.17, f32[64]{0:T(128)S(1)} %add_rsqrt_fusion.1, f32[4096]{0:T(1024)} %param.16, bf16[64,4096]{1,0:T(8,128)(2,1)S(1)} %all_gather.9), kind=kOutput, calls=%fused_computation.48 | convolution fusion | flops 269516736 | bytes 4866560 | tf_op jit(solution)/shard_map/dot_general | solution.py:33
  53.8 0.0 copy-start.2
  53.8 0.1 convert_element_type.30
  53.9 0.4 multiply_reduce_fusion.2
  54.3 0.0 copy-done.1
  54.3 0.2 copy-done.2
  54.5 1.6 %fusion.25 = (f32[2,64]{1,0:T(2,128)S(1)}, f32[2,64,512]{2,1,0:T(8,128)S(1)}) fusion(bf16[512,4096]{1,0:T(8,128)(2,1)S(1)} %copy-done.1, f32[4096]{0:T(1024)S(1)} %copy-done.2, f32[2,64]{1,0:T(2,128)S(1)} %get-tuple-element.17, f32[2,4096]{1,0:T(2,128)S(1)} %bitcast.17, f32[64,4096]{1,0:T(8,128)S(1)} %convert_element_type.30, f32[2,64]{1,0:T(2,128)S(1)} %psum.42), kind=kOutput, calls=%fused_computation.49 | convolution fusion | flops 539557760 | bytes 5555712 | tf_op jit(solution)/shard_map/etd,vd->etv/dot_general | solution.py:39
  56.1 18.6 %all-reduce.1 = (f32[64]{0:T(128)S(1)}, f32[2,64]{1,0:T(2,128)S(1)}) all-reduce(f32[64]{0:T(128)S(1)} %get-tuple-element.18, f32[2,64]{1,0:T(2,128)S(1)} %get-tuple-element.20), channel_id=1, replica_groups=mesh['groups'=2,'vocab'=4,'edit'=2,'tok'=2] {'vocab','edit'}, use_global_device_ids=true, to_apply=%region_8.0 | all-reduce | flops 192 | bytes 1536 | tf_op jit(solution)/shard_map/pmax | solution.py:45
  74.7 0.2 fusion.23
  74.9 0.2 multiply_reduce_fusion.4
  75.1 17.7 %all-reduce = (f32[64]{0:T(128)S(1)}, f32[2,64]{1,0:T(2,128)S(1)}, f32[2,64]{1,0:T(2,128)S(1)}, f32[2,64]{1,0:T(2,128)S(1)}) all-reduce(f32[64]{0:T(128)S(1)} %get-tuple-element.14, f32[2,64]{1,0:T(2,128)S(1)} %get-tuple-element.5, ...), channel_id=1, replica_groups=mesh['groups'=2,'vocab'=4,'edit'=2,'tok'=2] {'vocab','edit'}, use_global_device_ids=true, to_apply=%region_10.0 | all-reduce | flops 448 | bytes 3584 | tf_op jit(solution)/shard_map/psum | solution.py:51
  92.8 0.1 subtract_exponential_fusion
  92.9 0.5 constant_dynamic-slice_fusion
  93.4 3.4 %multiply_reduce_fusion.1 = (f32[2,64]{1,0:T(2,128)S(1)}, f32[2,64,4096]{2,1,0:T(8,128)S(1)}) fusion(f32[2,4096]{1,0:T(2,128)S(1)} %bitcast.18, f32[64,4096]{1,0:T(8,128)S(1)} %convert_element_type.30, f32[2,64]{1,0:T(2,128)S(1)} %psum.42, bf16[512,4096]{1,0:T(8,128)(2,1)} %param.17, f32[2,64,512]{2,1,0:T(8,128)S(1)} %get-tuple-element.21, ...), kind=kOutput, calls=%fused_computation.6 | convolution fusion | flops 539754368 | bytes 7784192 | tf_op jit(solution)/shard_map/etv,vd->etd/dot_general | solution.py:62
  96.9 0.8 multiply_reduce_fusion
  97.7 57.6 %psum.45 = f32[2,4096]{1,0:T(2,128)S(1)} all-reduce(f32[2,4096]{1,0:T(2,128)S(1)} %multiply_reduce_fusion), channel_id=1, replica_groups=mesh['groups'=2,'vocab'=4,'edit'=2,'tok'=2] {'vocab','edit','tok'}, use_global_device_ids=true, to_apply=%region_13.0 | all-reduce | flops 8192 | bytes 65536 | tf_op jit(solution)/shard_map/psum | solution.py:69
  155.3 0.7 dynamic_slice.10
  (8 shorter events, 0.1 us)
Async XLA Ops:
  0.6 1.0 copy-start
  49.9 4.4 %copy-start.1 = (bf16[512,4096]{1,0:T(8,128)(2,1)S(1)}, bf16[512,4096]{1,0:T(8,128)(2,1)}, u32[]{:S(2)}) copy-start(bf16[512,4096]{1,0:T(8,128)(2,1)} %param.17) | copy-start | bytes 12582916
  53.8 0.7 copy-start.2
where the time goes:
time: 156 us
  blocking collectives  140 us (90%)
  matrix products  10 us (6%)
  other arithmetic  3.51 us (2%)
  local copies, waits for them, and re-layouts  1.73 us (1%)
    psum x1, blocking collectives, per_device(): grad_total = lax.psum(grad_part, ('vocab', 'edit', 'tok'))  57.6 us
    pmax x1, blocking collectives, per_device(): peak_base, peak_edit = lax.pmax((peak_base, peak_edit), ('vocab', 'edit'))  18.6 us
    psum x1, blocking collectives, per_device(): lax.psum((base_total, edit_total, cross_sum, target), ('vocab', 'edit'))  17.7 us
    all_gather x1, blocking collectives, per_device(): lax.all_gather(base_out, 'vocab', axis=1, tiled=True)  15 us
    psum x1, blocking collectives, per_device(): coeff = lax.psum(coeff_part, 'vocab')  13.4 us
    all_gather x1, blocking collectives, per_device(): lax.all_gather(value_vecs, 'vocab', axis=1, tiled=True)  13.3 us
    all_gather x1, blocking collectives, per_device(): values = lax.all_gather(local_values, 'edit', axis=0, tiled=True)  4.4 us
    dot_general x1, matrix products, per_device(): lax.dot_general(base_norm, head, (((1,), (1,)), ((), ())), preferred_elem...  3.87 us

commit v1 on v0

--- a/solution.py
+++ b/solution.py
@@ -22,7 +22,10 @@
     coeff_part = lax.dot_general(
         edit_keys, hidden_act, (((1,), (1,)), ((), ())), preferred_element_type=jnp.float32
     )
-    coeff = lax.psum(coeff_part, "vocab")
+    n_dev, coeff = (lax.axis_size("vocab"), coeff_part)
+    for hop in [1 << k for k in range(n_dev.bit_length() - 1)]:
+        pairs = [(i, i ^ hop) for i in range(n_dev)]
+        coeff = coeff + lax.ppermute(coeff, "vocab", pairs)
     base_rows, local_values = (
         lax.all_gather(base_out, "vocab", axis=1, tiled=True),
         lax.all_gather(value_vecs, "vocab", axis=1, tiled=True),

time: 156 us -> 154 us (0.987)
  blocking collectives: 140 us -> 128 us
  starting transfers between devices: 0 us -> 3.85 us
  waiting for transfers between devices: 0 us -> 3.68 us
  matrix products: 10 us -> 12.1 us
    psum x1 -> x0, blocking collectives: 13.4 us -> none  [per_device(): coeff = lax.psum(coeff_part, 'vocab')]
    ppermute x0 -> x2, starting transfers between devices: none -> 3.85 us  [per_device(): coeff = coeff + lax.ppermute(coeff, 'vocab', pairs)]
    ppermute x0 -> x2, waiting for transfers between devices: none -> 3.68 us  [per_device(): coeff = coeff + lax.ppermute(coeff, 'vocab', pairs)]
    dot_general x1, matrix products: 1.62 us -> 3.82 us  [per_device(): jnp.einsum('etd,vd->etv', normed, head, preferred_element_type=jnp.float32)]
  transfers between devices with their start and end apart: 0 -> 2, of which waited for: 0 -> 1; matrix products, arithmetic and copies ran while one was open for 0% -> 3% of each run, Pallas kernels for 0% -> 0%
where the time goes in v1:
time: 154 us
  blocking collectives  128 us (83%)
  matrix products  12.1 us (8%)
  starting transfers between devices  3.85 us (2%)
  waiting for transfers between devices  3.68 us (2%)
  other arithmetic  2.81 us (2%)
  local copies, waits for them, and re-layouts  2.25 us (1%)
    psum x1, blocking collectives, per_device(): grad_total = lax.psum(grad_part, ('vocab', 'edit', 'tok'))  57.6 us
    pmax x1, blocking collectives, per_device(): peak_base, peak_edit = lax.pmax((peak_base, peak_edit), ('vocab', 'edit'))  19.9 us
    psum x1, blocking collectives, per_device(): lax.psum((base_total, edit_total, cross_sum, target), ('vocab', 'edit'))  17.1 us
    all_gather x1, blocking collectives, per_device(): lax.all_gather(base_out, 'vocab', axis=1, tiled=True)  15.5 us
    all_gather x1, blocking collectives, per_device(): lax.all_gather(value_vecs, 'vocab', axis=1, tiled=True)  13.5 us
    all_gather x1, blocking collectives, per_device(): values = lax.all_gather(local_values, 'edit', axis=0, tiled=True)  4.55 us
    ppermute x2, starting transfers between devices, per_device(): coeff = coeff + lax.ppermute(coeff, 'vocab', pairs)  3.85 us
    dot_general x1, matrix products, per_device(): jnp.einsum('etd,vd->etv', normed, head, preferred_element_type=jnp.float32)  3.82 us
  transfers between devices with their start and end apart: 2, of which 1 were waited for; matrix products, arithmetic and copies ran while one was open for 3% of the time, Pallas kernels for 0%

profile of v1, /device:TPU:0, one launch (start us, length us, event | category | flops | bytes accessed | tf_op | source)
XLA Modules:
  0.0 153.6 jit_solution(5780280906328307840)
XLA Ops:
  0.6 0.0 copy-start
  0.6 1.0 copy-done
  1.7 1.1 fusion.3
  2.8 3.0 %collective-permute-start = (f32[2,64]{1,0:T(2,128)S(1)}, f32[2,64]{1,0:T(2,128)S(1)}, u32[]{:S(2)}, u32[]{:S(2)}) collective-permute-start(f32[2,64]{1,0:T(2,128)S(1)} %fusion.3), channel_id=1, source_target_pairs={{0,4},{4,0},{8,12},{12,8},{1,5},{5,1},{9,13},{13,9},{2,6},{6,2},{1... | collective-permute-start | bytes 1544 | tf_op jit(solution)/shard_map/ppermute | solution.py:28
  5.9 13.5 %all_gather.10 = bf16[1,4096]{1,0:T(2,128)(2,1)S(1)} all-gather(bf16[1,1024]{1,0:T(2,128)(2,1)} %param.15), channel_id=1, replica_groups=mesh['groups'=2,'vocab'=4,'edit'=2,'tok'=2] {'vocab'}, dimensions={1}, use_global_device_ids=true | all-gather | bytes 10240 | tf_op jit(solution)/shard_map/all_gather | solution.py:31
  19.3 15.5 %all_gather.9 = bf16[64,4096]{1,0:T(8,128)(2,1)S(1)} all-gather(bf16[64,1024]{1,0:T(8,128)(2,1)} %param.14), channel_id=1, replica_groups=mesh['groups'=2,'vocab'=4,'edit'=2,'tok'=2] {'vocab'}, dimensions={1}, use_global_device_ids=true | all-gather | bytes 655360 | tf_op jit(solution)/shard_map/all_gather | solution.py:30
  34.8 0.2 multiply_reduce_fusion.3
  35.0 0.7 compare_convert_fusion
  35.7 0.0 copy-start.2
  35.8 3.7 %fusion.24 = (f32[64]{0:T(128)S(1)}, f32[64,512]{1,0:T(8,128)S(1)}) fusion(bf16[512,4096]{1,0:T(8,128)(2,1)} %param.17, f32[64]{0:T(128)S(1)} %add_rsqrt_fusion.1, f32[4096]{0:T(1024)} %param.16, bf16[64,4096]{1,0:T(8,128)(2,1)S(1)} %all_gather.9), kind=kOutput, calls=%fused_computation.48 | convolution fusion | flops 269516736 | bytes 4866560 | tf_op jit(solution)/shard_map/dot_general | solution.py:36
  39.5 0.0 copy-start.1
  39.5 4.5 %all-gather = bf16[2,1,4096]{2,1,0:T(2,128)(2,1)S(1)} all-gather(bf16[1,1,4096]{2,1,0:T(2,128)(2,1)S(1)} %bitcast.20), channel_id=1, replica_groups=mesh['groups'=2,'vocab'=4,'edit'=2,'tok'=2] {'edit'}, dimensions={0}, use_global_device_ids=true | all-gather | bytes 24576 | tf_op jit(solution)/shard_map/all_gather | solution.py:33
  44.0 0.1 convert_element_type.30
  44.1 0.0 collective-permute-done
  44.1 0.8 collective-permute-start.1
  44.9 0.0 copy-done.2
  45.0 3.7 %collective-permute-done.1 = f32[2,64]{1,0:T(2,128)S(1)} collective-permute-done((f32[2,64]{1,0:T(2,128)S(1)}, f32[2,64]{1,0:T(2,128)S(1)}, u32[]{:S(2)}, u32[]{:S(2)}) %collective-permute-start.1) | collective-permute-done | bytes 544 | tf_op jit(solution)/shard_map/ppermute | solution.py:28
  48.7 0.4 multiply_reduce_fusion.2
  49.1 0.0 copy-done.1
  49.1 3.8 %fusion.25 = (f32[2,64]{1,0:T(2,128)S(1)}, f32[2,64,512]{2,1,0:T(8,128)S(1)}) fusion(bf16[512,4096]{1,0:T(8,128)(2,1)} %param.17, f32[4096]{0:T(1024)S(1)} %copy-done.1, f32[2,64]{1,0:T(2,128)S(1)} %get-tuple-element.17, f32[2,4096]{1,0:T(2,128)S(1)} %bitcast.17, f32[64,4096]{1,0:T(8,128)S(1)} %convert_element_type.30, f32[2,64]{1,0:T(2,128)S(1)} %add.82), kind=kOutput, calls=%fused_computation.49 | convolution fusion | flops 539557760 | bytes 5555712 | tf_op jit(solution)/shard_map/etd,vd->etv/dot_general | solution.py:42
  53.0 19.9 %all-reduce.1 = (f32[64]{0:T(128)S(1)}, f32[2,64]{1,0:T(2,128)S(1)}) all-reduce(f32[64]{0:T(128)S(1)} %get-tuple-element.18, f32[2,64]{1,0:T(2,128)S(1)} %get-tuple-element.20), channel_id=1, replica_groups=mesh['groups'=2,'vocab'=4,'edit'=2,'tok'=2] {'vocab','edit'}, use_global_device_ids=true, to_apply=%region_7.0 | all-reduce | flops 192 | bytes 1536 | tf_op jit(solution)/shard_map/pmax | solution.py:48
  72.9 0.2 fusion.23
  73.1 0.2 multiply_reduce_fusion.4
  73.3 17.1 %all-reduce = (f32[64]{0:T(128)S(1)}, f32[2,64]{1,0:T(2,128)S(1)}, f32[2,64]{1,0:T(2,128)S(1)}, f32[2,64]{1,0:T(2,128)S(1)}) all-reduce(f32[64]{0:T(128)S(1)} %get-tuple-element.14, f32[2,64]{1,0:T(2,128)S(1)} %get-tuple-element.5, ...), channel_id=1, replica_groups=mesh['groups'=2,'vocab'=4,'edit'=2,'tok'=2] {'vocab','edit'}, use_global_device_ids=true, to_apply=%region_9.0 | all-reduce | flops 448 | bytes 3584 | tf_op jit(solution)/shard_map/psum | solution.py:54
  90.4 0.1 subtract_exponential_fusion
  90.6 3.4 %multiply_reduce_fusion.1 = (f32[2,64]{1,0:T(2,128)S(1)}, f32[2,64,4096]{2,1,0:T(8,128)S(1)}) fusion(f32[2,4096]{1,0:T(2,128)S(1)} %bitcast.18, f32[64,4096]{1,0:T(8,128)S(1)} %convert_element_type.30, f32[2,64]{1,0:T(2,128)S(1)} %add.82, bf16[512,4096]{1,0:T(8,128)(2,1)} %param.17, f32[2,64,512]{2,1,0:T(8,128)S(1)} %get-tuple-element.21, ...), kind=kOutput, calls=%fused_computation.6 | convolution fusion | flops 539754368 | bytes 7784192 | tf_op jit(solution)/shard_map/etv,vd->etd/dot_general | solution.py:65
  94.0 0.8 multiply_reduce_fusion
  94.8 57.6 %psum.37 = f32[2,4096]{1,0:T(2,128)S(1)} all-reduce(f32[2,4096]{1,0:T(2,128)S(1)} %multiply_reduce_fusion), channel_id=1, replica_groups=mesh['groups'=2,'vocab'=4,'edit'=2,'tok'=2] {'vocab','edit','tok'}, use_global_device_ids=true, to_apply=%region_12.0 | all-reduce | flops 8192 | bytes 65536 | tf_op jit(solution)/shard_map/psum | solution.py:72
  152.4 0.5 constant_dynamic-slice_fusion
  152.9 0.7 dynamic_slice.10
  (11 shorter events, 0.1 us)
Async XLA Ops:
  0.6 1.0 copy-start
  2.8 41.3 %collective-permute-start = (f32[2,64]{1,0:T(2,128)S(1)}, f32[2,64]{1,0:T(2,128)S(1)}, u32[]{:S(2)}, u32[]{:S(2)}) collective-permute-start(f32[2,64]{1,0:T(2,128)S(1)} %fusion.3), channel_id=1, source_target_pairs={{0,4},{4,0},{8,12},{12,8},{1,5},{5,1},{9,13},{13,9},{2,6},{6,2},{1... | collective-permute-start | bytes 1544 | tf_op jit(solution)/shard_map/ppermute | solution.py:28
  35.7 9.2 %copy-start.2 = (s32[64]{0:T(128)S(1)}, s32[64]{0:T(128)}, u32[]{:S(2)}) copy-start(s32[64]{0:T(128)} %param.10) | copy-start | bytes 772
  39.5 9.7 %copy-start.1 = (f32[4096]{0:T(1024)S(1)}, f32[4096]{0:T(1024)}, u32[]{:S(2)}) copy-start(f32[4096]{0:T(1024)} %param.16) | copy-start | bytes 49156
  44.1 4.5 %collective-permute-start.1 = (f32[2,64]{1,0:T(2,128)S(1)}, f32[2,64]{1,0:T(2,128)S(1)}, u32[]{:S(2)}, u32[]{:S(2)}) collective-permute-start(f32[2,64]{1,0:T(2,128)S(1)} %add.81), channel_id=1, source_target_pairs={{0,8},{4,12},{8,0},{12,4},{1,9},{5,13},{9,1},{13,5},{2,10},{6,14},... | collective-permute-start | bytes 1544 | tf_op jit(solution)/shard_map/ppermute | solution.py:28
